TPU v7x, 32 devices: a whole 2x2x4 slice. The times are simulated.
32 devices in a mesh: az: 8 (over y, x, core), rg: 4 (over z).
Axes of the slice: x: 2, y: 2, z: 4, core: 2. Of those that a mesh axis runs over, the one named last changes fastest.
Arguments:
- reference_slc: bfloat16 [2, 768, 12288], P(None, 'az', 'rg'), may hold values from -6 to 6
- secondary_slc: bfloat16 [2, 768, 12288], P(None, 'az', 'rg'), may hold values from -6 to 6
- chip_offsets: int32 [2, 8, 384], P(None, 'az', 'rg'), may hold values from -80 to 80, as said below
- src_row: int32 [768], replicated, may hold values from 0 to 767, as said below
- line_owner: int32 [768], replicated, may hold values from 0 to 31, as said below
- band_start: int32 [12288], replicated, may hold values from -64 to 12343, as said below
- band_taps: bfloat16 [8, 12288], replicated, may hold values from -2.09375 to 2.09375
Outputs:
- est_offsets: float32 [2, 8, 384], P(None, 'az', 'rg')
- resampled: bfloat16 [2, 1024, 12288], P(None, ('az', 'rg'))
Inputs may be any that keep to these rules, and one draw needn't show every extreme that they name: chip_offsets[0] lies within -80 and 80, chip_offsets[1] within -48 and 48. `src_row`: the source row of line i lies within 8 rows of i. `line_owner`: for every owner and every azimuth tile, at most 4 lines of that owner take their source rows from that tile, and an owner holds at most 32 lines; both bounds are met in every draw. band_start[j] lies within j - 64 and j + 56.
All inputs are finite; a program needn't handle non-finite values.
Results may differ from a plain program's by a relative error of at most 0.008.
Values may be sent and summed in bfloat16 or wider, within the bound.
A program may use at most 128 MiB of HBM per device.

v0:
```python
import functools
import math

import jax
import jax.numpy as jnp
import numpy as np
from jax import lax
from jax.experimental import pallas as pl
from jax.experimental.pallas import tpu as pltpu
from jax.sharding import PartitionSpec as P

CHIP_LEN = 64
OVERSAMPLE = 16
LAG_COUNT = 48
TAP_COUNT = 8
SPACING = 32
MARGIN = 64
MAX_SHIFT = 8
LANES = 128
GROUP = 8

PHASE_RATE = 2.0
EPS = 1e-06
VMEM_LIMIT = 56 * 1024 * 1024


def make_tables():
    indices = np.arange(CHIP_LEN)
    product = indices[:, None] * indices[None, :] % CHIP_LEN
    angles = (-2.0 * math.pi / CHIP_LEN) * product
    scaling = 1.0 / math.sqrt(CHIP_LEN)
    four_re = np.cos(angles) * scaling
    four_im = np.sin(angles) * scaling
    lag_steps = np.arange(LAG_COUNT) - LAG_COUNT // 2
    frequency = np.where(indices < CHIP_LEN // 2, indices, indices - CHIP_LEN)
    phase_turns = lag_steps[:, None] * frequency[None, :] % (OVERSAMPLE * CHIP_LEN)
    lifted = 2.0 * math.pi / (OVERSAMPLE * CHIP_LEN) * phase_turns
    lift_re = np.cos(lifted) * scaling
    lift_im = np.sin(lifted) * scaling
    lag_values = (lag_steps / OVERSAMPLE).astype(np.float32)

    def left(re, im):
        return np.block([[re, -im], [im, re]])

    def right(re, im):
        pad = ((0, CHIP_LEN - re.shape[0]), (0, 0))
        re2 = np.kron(np.eye(2), np.pad(re, pad).T)
        im2 = np.kron(np.eye(2), np.pad(im, pad).T)
        return np.block([[re2, im2], [-im2, re2]])

    def held(table):
        return jnp.asarray(table.astype(np.float32)).astype(jnp.bfloat16)

    return (
        held(left(four_re, four_im)),
        held(right(four_re, four_im)),
        held(right(lift_re, lift_im)),
        held(left(lift_re, lift_im)),
        lag_values,
    )


def dot(a, b):
    return jnp.dot(a, b, preferred_element_type=jnp.float32)


ROWS = 16
CHUNK = 512


def place_bands(rel_ref, taps_ref, bands):
    place = lax.broadcasted_iota(jnp.int32, (2 * LANES, LANES), 0)

    def step(b, carry):
        cols = pl.ds(pl.multiple_of(b * LANES, LANES), LANES)
        delta = place - rel_ref[0:1, cols]
        taps = taps_ref[:, cols].astype(jnp.float32)
        band = jnp.zeros((2 * LANES, LANES), jnp.float32)
        for t in range(TAP_COUNT):
            band = jnp.where(delta == t, taps[t : t + 1], band)
        bands[b] = band.astype(jnp.bfloat16)
        return carry

    lax.fori_loop(0, bands.shape[0], step, 0)


def fill_windows(ref_ref, sec_ref, halos, ref_win, sec_win):
    top, low, left, right, ref_left, ref_right, top_left, top_right, low_left, low_right = halos
    lines = sec_ref.shape[1]
    blocks = sec_ref.shape[2] // LANES
    first = lines // 2 - CHIP_LEN // 2
    high = MARGIN + lines
    f32 = jnp.float32
    for c in range(2):
        for b in range(blocks):
            at = slice(b * LANES, (b + 1) * LANES)
            ref_win[c, b + 1] = ref_ref[c, first : first + CHIP_LEN, at].astype(f32)
            sec_win[c, b + 1, :MARGIN] = top[c, :, at].astype(f32)
            sec_win[c, b + 1, MARGIN:high] = sec_ref[c, :, at].astype(f32)
            sec_win[c, b + 1, high:] = low[c, :, at].astype(f32)
        ref_win[c, 0] = ref_left[c].astype(f32)
        ref_win[c, blocks + 1] = ref_right[c].astype(f32)
        for b, (above, beside, below) in (
            (0, (top_left, left, low_left)),
            (blocks + 1, (top_right, right, low_right)),
        ):
            sec_win[c, b, :MARGIN] = above[c].astype(f32)
            sec_win[c, b, MARGIN:high] = beside[c].astype(f32)
            sec_win[c, b, high:] = below[c].astype(f32)


def estimate(off_ref, tables, base_ref, ref_win, sec_win, plain_ref, lagged_ref, est_ref):
    four_ref, spec_ref, lift_ref, corr_ref, lag_ref, wide_ref = tables
    chips = off_ref.shape[1]
    lines = sec_win.shape[2] - 2 * MARGIN
    rim = (CHIP_LEN - SPACING) // 2
    first = lines // 2 - CHIP_LEN // 2
    lane = lax.broadcasted_iota(jnp.int32, (CHIP_LEN, LANES), 1)

    def placed(win, c, row, col, half):
        block = col // LANES
        inner = col - block * LANES
        near = win[c, block, pl.ds(row, CHIP_LEN), :]
        far = win[c, block + 1, pl.ds(row, CHIP_LEN), :]
        turn = (half * CHIP_LEN - inner + LANES) % LANES
        near = pltpu.roll(near, turn, 1)
        far = pltpu.roll(far, turn, 1)
        return jnp.where(lane - half * CHIP_LEN + inner < LANES, near, far)

    def pair(win, rows, cols_at):
        parts = []
        for c in range(2):
            even = placed(win, c, rows[0], cols_at[0], 0)
            odd = placed(win, c, rows[1], cols_at[1], 1)
            parts.append(jnp.where(lane < CHIP_LEN, even, odd).astype(jnp.bfloat16))
        return jnp.concatenate(parts, axis=0)

    def step(i, carry):
        ref_chips, sec_chips = [], []
        for j in range(GROUP):
            g = (i * GROUP + j) * 2
            at = [LANES + SPACING * (g + h) - rim for h in range(2)]
            ref_chips.append(pair(ref_win, (0, 0), at))
            rows = [MARGIN + first + off_ref[0, g + h] for h in range(2)]
            sec_chips.append(pair(sec_win, rows, [at[h] + off_ref[1, g + h] for h in range(2)]))
        both = jnp.concatenate(ref_chips + sec_chips, axis=1)
        half = dot(four_ref[...], both).astype(jnp.bfloat16)
        lhs = jnp.concatenate(
            [
                jnp.concatenate(
                    [
                        half[:CHIP_LEN, j * LANES : (j + 1) * LANES],
                        half[CHIP_LEN:, j * LANES : (j + 1) * LANES],
                    ],
                    axis=1,
                )
                for j in range(2 * GROUP)
            ],
            axis=0,
        )
        spec = dot(lhs, spec_ref[...])
        rows = GROUP * CHIP_LEN
        rr, ri = spec[:rows, :LANES], spec[:rows, LANES:]
        sr, si = spec[rows:, :LANES], spec[rows:, LANES:]
        cross = jnp.concatenate([rr * sr + ri * si, ri * sr - rr * si], axis=1)
        mid = dot(cross.astype(jnp.bfloat16), lift_ref[...]).astype(jnp.bfloat16)
        tall = jnp.concatenate(
            [
                jnp.concatenate(
                    [
                        mid[j * CHIP_LEN : (j + 1) * CHIP_LEN, :LANES],
                        mid[j * CHIP_LEN : (j + 1) * CHIP_LEN, LANES:],
                    ],
                    axis=0,
                )
                for j in range(GROUP)
            ],
            axis=1,
        )
        corr = dot(corr_ref[...], tall)
        energy = corr[:LAG_COUNT] * corr[:LAG_COUNT] + corr[LAG_COUNT:] * corr[LAG_COUNT:]
        weight = energy * energy
        plain = jnp.sum(weight, axis=0, keepdims=True)
        lagged = jnp.sum(weight * lag_ref[...], axis=0, keepdims=True)
        for j in range(GROUP):
            at = slice(j * LANES, (j + 1) * LANES)
            plain_ref[pl.ds(i * GROUP + j, 1), :] = plain[:, at]
            lagged_ref[pl.ds(i * GROUP + j, 1), :] = lagged[:, at]
        return carry

    lax.fori_loop(0, chips // (2 * GROUP), step, 0)
    near = lax.broadcasted_iota(jnp.int32, (chips // 2, LANES), 1) < CHIP_LEN
    plain = plain_ref[...]
    lagged = lagged_ref[...]
    across = plain * wide_ref[...]
    lane = lax.broadcasted_iota(jnp.int32, (chips // 2, LANES), 1)
    place = lax.broadcasted_iota(jnp.int32, (chips // 2, LANES), 0) * 2
    rows = [jnp.zeros((chips // 2, LANES), jnp.float32)] * 2
    for h in range(2):
        inside = near if h == 0 else jnp.logical_not(near)
        total = jnp.sum(jnp.where(inside, plain, 0.0), axis=1, keepdims=True) + EPS
        for c, moment in enumerate((lagged, across)):
            centre = jnp.sum(jnp.where(inside, moment, 0.0), axis=1, keepdims=True) / total
            rows[c] = jnp.where(lane == place + h, centre, rows[c])
    for c in range(2):
        est_ref[c : c + 1, :] = jnp.sum(rows[c], axis=0, keepdims=True) + base_ref[c : c + 1, :]


def fused_kernel(
    group_rows, far_first, off_ref, ref_ref, sec_ref, send_pick, recv_pick, rel_ref, taps_ref,
    tile_ref, four_ref, spec_ref, lift_ref, corr_ref, lag_ref, wide_ref, base_ref, est_ref,
    out_ref, outgoing, arrived, top, low, left, right, ref_left, ref_right, top_left, top_right,
    low_left, low_right, ref_win, sec_win, plain_ref, lagged_ref, bands, wide, mine, everyone,
    halo_send, halo_recv, bulk_send, bulk_recv, est_send, est_recv,
):
    az_count = lax.axis_size("az")
    rg_count = lax.axis_size("rg")
    az = lax.axis_index("az")
    rg = lax.axis_index("rg")
    me = az * rg_count + rg
    owners = az_count * rg_count
    lines = sec_ref.shape[1]
    cols = sec_ref.shape[2]
    groups = ROWS // group_rows
    part = cols // groups
    first = lines // 2 - CHIP_LEN // 2
    mesh_ids = pl.DeviceIdType.MESH

    def for_others(body):
        def plane(d, carry):
            def one(k, inner):
                body((az + k) % az_count, (rg + d) % rg_count)
                return inner

            return lax.fori_loop(jnp.where(d == 0, 1, 0), az_count, one, carry)

        lax.fori_loop(0, rg_count, plane, 0)

    barrier = pltpu.get_barrier_semaphore()

    def greet(a, r):
        pl.semaphore_signal(barrier, inc=1, device_id=(a, r), device_id_type=mesh_ids)

    for_others(greet)

    rows = jnp.concatenate([sec_ref[0], sec_ref[1]], axis=0)
    for at in range(0, part, CHUNK):
        width = min(CHUNK, part - at)
        picked = [
            dot(send_pick[g], rows[:, g * part + at : g * part + at + width])
            for g in range(send_pick.shape[0])
        ]
        if group_rows == 8:
            picked = [
                dot(send_pick[0], rows[:, g * part + at : g * part + at + width]).reshape(
                    owners, group_rows, width
                )
                for g in range(groups)
            ]
            tall = jnp.concatenate(picked, axis=1)
        else:
            tall = sum(picked).reshape(owners, ROWS, width)
        outgoing[:, :, at : at + width] = tall.astype(jnp.bfloat16)

    pl.semaphore_wait(barrier, owners - 1)

    high = lines - MARGIN
    last = cols - LANES
    middle = pl.ds(first, CHIP_LEN)
    moves = (
        (1, 0, sec_ref.at[:, pl.ds(high, MARGIN), :], top),
        (-1, 0, sec_ref.at[:, pl.ds(0, MARGIN), :], low),
        (0, 1, sec_ref.at[:, :, pl.ds(last, LANES)], left),
        (0, -1, sec_ref.at[:, :, pl.ds(0, LANES)], right),
        (0, 1, ref_ref.at[:, middle, pl.ds(last, LANES)], ref_left),
        (0, -1, ref_ref.at[:, middle, pl.ds(0, LANES)], ref_right),
        (1, 1, sec_ref.at[:, pl.ds(high, MARGIN), pl.ds(last, LANES)], top_left),
        (1, -1, sec_ref.at[:, pl.ds(high, MARGIN), pl.ds(0, LANES)], top_right),
        (-1, 1, sec_ref.at[:, pl.ds(0, MARGIN), pl.ds(last, LANES)], low_left),
        (-1, -1, sec_ref.at[:, pl.ds(0, MARGIN), pl.ds(0, LANES)], low_right),
    )

    def inside(a, r):
        return (a >= 0) & (a < az_count) & (r >= 0) & (r < rg_count)

    def halo(which):
        step_a, step_r, source, target = moves[which]
        return pltpu.make_async_remote_copy(
            src_ref=source,
            dst_ref=target,
            send_sem=halo_send.at[which],
            recv_sem=halo_recv.at[which],
            device_id=(
                (az + step_a + az_count) % az_count,
                (rg + step_r + rg_count) % rg_count,
            ),
            device_id_type=mesh_ids,
        )

    for which, (step_a, step_r, _, target) in enumerate(moves):
        @pl.when(inside(az + step_a, rg + step_r))
        def _():
            halo(which).start()

        @pl.when(jnp.logical_not(inside(az - step_a, rg - step_r)))
        def _():
            target[...] = jnp.zeros_like(target)

    def bulk(d):
        to = (rg + d) % rg_count

        def one(k, carry):
            a = (az + k) % az_count
            pltpu.make_async_remote_copy(
                src_ref=outgoing.at[a * rg_count + to],
                dst_ref=arrived.at[rg, az],
                send_sem=bulk_send,
                recv_sem=bulk_recv.at[d],
                device_id=(a, to),
                device_id_type=mesh_ids,
            ).start()
            return carry

        lax.fori_loop(1 if d == 0 else 0, az_count, one, 0)

    for d in far_first:
        bulk(d)
    arrived[rg, az] = outgoing[az * rg_count + rg]

    place_bands(rel_ref, taps_ref, bands)

    for which, (step_a, step_r, _, _) in enumerate(moves):
        @pl.when(inside(az - step_a, rg - step_r))
        def _():
            halo(which).wait_recv()

    halos = (
        top, low, left, right, ref_left, ref_right, top_left, top_right, low_left, low_right
    )
    fill_windows(ref_ref, sec_ref, halos, ref_win, sec_win)
    tables = (four_ref, spec_ref, lift_ref, corr_ref, lag_ref, wide_ref)
    estimate(off_ref, tables, base_ref, ref_win, sec_win, plain_ref, lagged_ref, est_ref)
    mine[...] = est_ref[0:1, :]
    everyone[me] = est_ref[0:1, :]

    def tell(a, r):
        pltpu.make_async_remote_copy(
            src_ref=mine,
            dst_ref=everyone.at[me],
            send_sem=est_send,
            recv_sem=est_recv,
            device_id=(a, r),
            device_id_type=mesh_ids,
        ).start()

    for_others(tell)

    owned = out_ref.shape[1]
    per_plane = cols // LANES
    wide[0, :, :MARGIN] = jnp.zeros((2 * owned, MARGIN), jnp.bfloat16)
    wide[rg_count - 1, :, MARGIN + cols :] = jnp.zeros((2 * owned, MARGIN), jnp.bfloat16)
    told = everyone.at[pl.ds(0, owners - 1)]
    pltpu.make_async_copy(told, told, est_recv).wait()

    lane = lax.broadcasted_iota(jnp.int32, (owned, LANES), 1) // SPACING
    tile = tile_ref[...]

    def turns(plane):
        angle = jnp.zeros((owned, LANES), jnp.float32)
        for a in range(az_count):
            angle = jnp.where(tile == a, everyone[a * rg_count + plane], angle)
        angle = PHASE_RATE * angle
        return jnp.cos(angle), jnp.sin(angle)

    def finish(plane, k, cosine, sine):
        b = plane * per_plane + k
        cols_at = pl.ds(pl.multiple_of(b * LANES, LANES), LANES)
        window = wide[plane, :, pl.ds(pl.multiple_of(k * LANES, LANES), 2 * LANES)]
        s = dot(window, bands[b])
        chip = lane + k * (LANES // SPACING)
        cos_k = jnp.take_along_axis(cosine, chip, axis=1)
        sin_k = jnp.take_along_axis(sine, chip, axis=1)
        s_re = s[:owned]
        s_im = s[owned:]
        out_ref[0, :, cols_at] = (s_re * cos_k + s_im * sin_k).astype(jnp.bfloat16)
        out_ref[1, :, cols_at] = (s_im * cos_k - s_re * sin_k).astype(jnp.bfloat16)

    for d in far_first:
        plane = (rg + rg_count - d) % rg_count
        landed = arrived.at[plane]
        if d == 0:
            landed = landed.at[pl.ds(0, az_count - 1)]
        pltpu.make_async_copy(landed, landed, bulk_recv.at[d]).wait()
        held = arrived[plane].reshape(az_count * ROWS, part)
        for g in range(groups):
            at = MARGIN + g * part
            wide[plane, :, at : at + part] = dot(recv_pick[g], held).astype(jnp.bfloat16)

        @pl.when(plane > 0)
        def _():
            wide[plane - 1, :, MARGIN + cols :] = wide[plane, :, MARGIN : 2 * MARGIN]

        @pl.when(plane < rg_count - 1)
        def _():
            wide[plane + 1, :, :MARGIN] = wide[plane, :, cols : MARGIN + cols]

        cosine, sine = turns(plane)
        inner = per_plane - 2
        unroll = next(u for u in (11, 10, 8, 7, 6, 5, 4, 3, 2, 1) if inner % u == 0)

        def some(i, carry):
            for j in range(unroll):
                finish(plane, 1 + i * unroll + j, cosine, sine)
            return carry

        lax.fori_loop(0, inner // unroll, some, 0)

    def edges(plane, carry):
        cosine, sine = turns(plane)
        finish(plane, 0, cosine, sine)
        finish(plane, per_plane - 1, cosine, sine)
        return carry

    lax.fori_loop(0, rg_count, edges, 0)

    for which, (step_a, step_r, _, _) in enumerate(moves):
        @pl.when(inside(az + step_a, rg + step_r))
        def _():
            halo(which).wait_send()

    gone = outgoing.at[pl.ds(0, owners - 1)]
    pltpu.make_async_copy(gone, gone, bulk_send).wait()
    pltpu.make_async_copy(told, told, est_send).wait()


def fused(offsets, ref, sec, send_pick, recv_pick, rel, taps, tile, tables, az_count, rg_count,
          owner_cap, group_rows):
    four, spec, lift, corr, lags = tables
    lines = sec.shape[1]
    cols = sec.shape[2]
    chips = cols // SPACING
    blocks = cols // LANES
    owners = az_count * rg_count
    part = cols * group_rows // ROWS
    far_first = sorted(range(1, rg_count), key=lambda d: abs(d - rg_count // 2)) + [0]
    vmem = pl.BlockSpec(memory_space=pltpu.VMEM)
    lag_wide = np.tile(np.pad(lags, (0, CHIP_LEN - LAG_COUNT)), 2)[None, :]
    bf16 = jnp.bfloat16
    f32 = jnp.float32
    args = (
        offsets, ref, sec, send_pick, recv_pick, rel, taps, tile, four, spec, lift, corr,
        jnp.asarray(lags)[:, None], jnp.asarray(lag_wide),
        jnp.pad(offsets, ((0, 0), (0, LANES - chips))).astype(f32),
    )
    return pl.pallas_call(
        functools.partial(fused_kernel, group_rows, tuple(far_first)),
        in_specs=[pl.BlockSpec(memory_space=pltpu.SMEM)] + [vmem] * (len(args) - 1),
        out_specs=(vmem, vmem),
        out_shape=(
            jax.ShapeDtypeStruct((2, LANES), f32),
            jax.ShapeDtypeStruct((2, owner_cap, cols * rg_count), bf16),
        ),
        scratch_shapes=[
            pltpu.VMEM((owners, ROWS, part), bf16),
            pltpu.VMEM((rg_count, az_count, ROWS, part), bf16),
            pltpu.VMEM((2, MARGIN, cols), bf16),
            pltpu.VMEM((2, MARGIN, cols), bf16),
            pltpu.VMEM((2, lines, LANES), bf16),
            pltpu.VMEM((2, lines, LANES), bf16),
            pltpu.VMEM((2, CHIP_LEN, LANES), bf16),
            pltpu.VMEM((2, CHIP_LEN, LANES), bf16),
            pltpu.VMEM((2, MARGIN, LANES), bf16),
            pltpu.VMEM((2, MARGIN, LANES), bf16),
            pltpu.VMEM((2, MARGIN, LANES), bf16),
            pltpu.VMEM((2, MARGIN, LANES), bf16),
            pltpu.VMEM((2, blocks + 3, CHIP_LEN, LANES), f32),
            pltpu.VMEM((2, blocks + 3, lines + 2 * MARGIN, LANES), f32),
            pltpu.VMEM((chips // 2, LANES), f32),
            pltpu.VMEM((chips // 2, LANES), f32),
            pltpu.VMEM((cols * rg_count // LANES, 2 * LANES, LANES), bf16),
            pltpu.VMEM((rg_count, 2 * owner_cap, cols + 2 * MARGIN), bf16),
            pltpu.VMEM((1, LANES), f32),
            pltpu.VMEM((owners, 1, LANES), f32),
            pltpu.SemaphoreType.DMA((10,)),
            pltpu.SemaphoreType.DMA((10,)),
            pltpu.SemaphoreType.DMA,
            pltpu.SemaphoreType.DMA((rg_count,)),
            pltpu.SemaphoreType.DMA,
            pltpu.SemaphoreType.DMA,
        ],
        compiler_params=pltpu.CompilerParams(
            vmem_limit_bytes=VMEM_LIMIT, collective_id=0, has_side_effects=True
        ),
        name="fused",
    )(*args)


def per_device(
    reference_slc, secondary_slc, chip_offsets, src_row, line_owner, band_start, band_taps
):
    tables = make_tables()
    lines_dev = secondary_slc.shape[1]
    cols_dev = secondary_slc.shape[2]
    chip_count = cols_dev // SPACING
    az_count = lax.axis_size("az")
    rg_count = lax.axis_size("rg")
    owners = az_count * rg_count
    pair_cap = max(2, (lines_dev + 2 * MAX_SHIFT + owners - 1) // owners)
    owner_cap = pair_cap * az_count
    group_rows = 2 * pair_cap
    groups = ROWS // group_rows
    total_cols = cols_dev * rg_count
    az_index = lax.axis_index("az")
    rg_index = lax.axis_index("rg")
    me_owner = az_index * rg_count + rg_index

    count = src_row.shape[0]
    ids = jnp.arange(count, dtype=jnp.int32)
    src_tile = src_row // lines_dev
    mine = (line_owner[:, None] == line_owner[None, :]) & (ids[:, None] < ids[None, :])
    own_rank = jnp.sum(mine.astype(jnp.int32), axis=0)
    near = mine & (src_tile[:, None] == src_tile[None, :])
    pair_rank = jnp.sum(near.astype(jnp.int32), axis=0)

    local_row = src_row - az_index * lines_dev
    slot = jnp.where(src_tile == az_index, line_owner * pair_cap + pair_rank, -1)
    slots = jnp.arange(owners * pair_cap, dtype=jnp.int32)
    send_row = jnp.sum(
        jnp.where(slots[:, None] == slot[None, :], local_row[None, :] + 1, 0), axis=1
    ) - 1
    send_row = send_row.reshape(owners, 1, pair_cap)
    part = jnp.arange(2, dtype=jnp.int32)[None, :, None] * lines_dev
    target = jnp.where(send_row >= 0, send_row + part, -1).reshape(owners, 1, group_rows)
    if group_rows == 8:
        target = target.reshape(1, owners * group_rows)
    else:
        group = jnp.arange(groups, dtype=jnp.int32)
        at_group = group[:, None, None, None] == group[None, None, :, None]
        target = jnp.where(at_group, target[None], -1).reshape(groups, owners * ROWS)
    send_pick = (
        target[:, :, None] == jnp.arange(2 * lines_dev, dtype=jnp.int32)[None, None, :]
    ).astype(jnp.bfloat16)

    all_cols = jnp.arange(total_cols, dtype=jnp.int32)
    rel = (band_start - all_cols // LANES * LANES + MARGIN)[None, :]

    outs = jnp.arange(owner_cap, dtype=jnp.int32)
    placed = (own_rank[None, :] == outs[:, None]) & (line_owner == me_owner)[None, :]
    which = jnp.sum(
        jnp.where(placed, (src_tile * pair_cap + pair_rank + 1)[None, :], 0), axis=1
    ) - 1
    tile = which // pair_cap
    from_rank = which % pair_cap
    group = jnp.arange(groups, dtype=jnp.int32)[:, None, None]
    parts = jnp.arange(2, dtype=jnp.int32)[None, :, None]
    source = (tile * ROWS + from_rank)[None, None] + group * group_rows + parts * pair_cap
    source = jnp.where(which[None, None] >= 0, source, -1).reshape(groups, 2 * owner_cap)
    recv_pick = (
        source[:, :, None] == jnp.arange(az_count * ROWS, dtype=jnp.int32)[None, None, :]
    ).astype(jnp.bfloat16)
    tile_wide = jnp.broadcast_to(tile[:, None], (owner_cap, LANES))

    est, lines_out = fused(
        chip_offsets[:, 0], reference_slc, secondary_slc, send_pick, recv_pick, rel, band_taps,
        tile_wide, tables, az_count, rg_count, owner_cap, group_rows,
    )
    return (est[:, None, :chip_count], lines_out)


def solution(mesh):
    return jax.shard_map(
        per_device,
        mesh=mesh,
        in_specs=(
            P(None, "az", "rg"),
            P(None, "az", "rg"),
            P(None, "az", "rg"),
            P(),
            P(),
            P(),
            P(),
        ),
        out_specs=(P(None, "az", "rg"), P(None, ("az", "rg"), None)),
        check_vma=False,
    )
```

profile of v0, /device:TPU:0, one launch (start us, length us, event | category | flops | bytes accessed | tf_op | source)
XLA Modules:
  0.0 71.5 jit_solution(16325293656444103574)
XLA Ops:
  0.6 0.7 broadcast_compare_fusion.1
  1.3 0.1 add.150
  1.4 0.1 add.151
  1.5 1.2 %pad_convert_fusion.base_ref = f32[2,128]{1,0:T(2,128)} fusion(s32[2,96]{1,0:T(2,128)} %bitcast.7), kind=kLoop, calls=%fused_computation.38 | loop fusion | flops 256 | bytes 1792 | tf_op jit(solution)/shard_map/convert_element_type | solution.py:453
  2.7 0.7 add_select_fusion.2
  3.4 1.2 %convert_reduce_fusion = (s32[768]{0:T(1024)S(1)}, s32[768]{0:T(1024)S(1)}) fusion(s32[768]{0:T(1024)} %param.17, s32[768]{0:T(1024)S(1)} %add_select_fusion.2), kind=kLoop, calls=%fused_computation | loop fusion | flops 5306880 | bytes 12288 | tf_op jit(solution)/shard_map/reduce_sum | solution.py:521
  4.7 0.7 %add_add_fusion = (s32[768]{0:T(1024)S(1)}, s32[768]{0:T(1024)S(1)}, s32[768]{0:T(1024)S(1)}) fusion(s32[768]{0:T(1024)S(1)} %get-tuple-element.13, s32[768]{0:T(1024)} %param.16, s32[768]{0:T(1024)} %param.17, s32[]{:T(128)S(6)} %axis_index.23, s32[]{:T(128)S(6)} %mul.51), kind=kLoop, calls=%fused_computation.26 | loop fusion | flops 13056 | bytes 18440 | tf_op jit(solution)/shard_map/add | solution.py:550
  5.4 0.1 select_reduce_fusion.1
  5.5 0.1 broadcast_in_dim.96
  5.6 0.1 select_reduce_fusion
  5.8 0.1 broadcast_add_fusion
  5.9 0.1 add.149
  5.9 0.1 sub.41
  6.1 0.1 add_select_fusion.1
  6.2 0.1 select_n.69
  6.3 0.7 broadcast_in_dim.100.tile_ref
  6.9 0.7 fusion.3.recv_pick
  7.6 1.4 %fusion.6 = s32[12288]{0:T(1024)} fusion(s32[12288]{0:T(1024)} %param.18), kind=kLoop, calls=%fused_computation.19 | loop fusion | flops 135168 | bytes 98304 | tf_op jit(solution)/shard_map/add | solution.py:545
  9.1 0.8 %fusion.1.send_pick = bf16[1,256,192]{2,1,0:T(8,128)(2,1)} fusion(s32[256]{0:T(256)S(1)} %select_n.69), kind=kLoop, calls=%fused_computation.7 | loop fusion | flops 98304 | bytes 99328 | tf_op jit(solution)/shard_map/convert_element_type | solution.py:542
  9.8 57.8 %fused.1 = (f32[2,128]{1,0:T(2,128)}, bf16[2,32,12288]{2,1,0:T(8,128)(2,1)}) custom-call(s32[2,96]{1,0:T(2,128)} %bitcast.8, bf16[2,96,3072]{2,1,0:T(8,128)(2,1)} %ref_ref.1, bf16[2,96,3072]{2,1,0:T(8,128)(2,1)} %sec_ref.1, bf16[1,256,192]{2,1,0:T(8,128)(2,1)} %fusion.1.send_pick, bf16[2,64,128]{2,1,0:T(8,128)(2,1)} %fusion.3.recv_pick, s32[1,12288]{1,0:T(1,128)} %bitcast.6, ...), custom_call_target="tpu_custom_call" | custom-call | tf_op jit(solution)/shard_map/fused/pallas_call | solution.py:455
  67.6 1.2 %copy.20 = f32[2,1,96]{2,1,0:T(1,128)} copy(f32[2,1,96]{2,1,0:T(1,128)} %bitcast.9) | data formatting | bytes 1536
  68.9 2.7 %copy.21 = bf16[2,32,12288]{2,1,0:T(8,128)(2,1)} copy(bf16[2,32,12288]{2,1,0:T(8,128)(2,1)} %get-tuple-element.22) | data formatting | bytes 3145728
  (10 shorter events, 0.1 us)
where the time goes:
time: 71.9 us; the launch traced here: 71.5 us
  Pallas kernels  57.8 us (80%)
  other arithmetic  7.91 us (11%)
  local copies, waits for them, and re-layouts  5.09 us (7%)
    pallas_call x1, Pallas kernels, fused(): pl.pallas_call(functools.partial(fused_kernel, group_rows, tuple(far_firs...  57.8 us
    unnamed x2, local copies, waits for them, and re-layouts  3.87 us

commit v1 on v0

--- a/solution.py
+++ b/solution.py
@@ -68,12 +68,12 @@
 CHUNK = 512
 
 
-def place_bands(rel_ref, taps_ref, bands):
+def place_bands(start_ref, taps_ref, bands):
     place = lax.broadcasted_iota(jnp.int32, (2 * LANES, LANES), 0)
 
     def step(b, carry):
         cols = pl.ds(pl.multiple_of(b * LANES, LANES), LANES)
-        delta = place - rel_ref[0:1, cols]
+        delta = place - (start_ref[0:1, cols] - b * LANES + MARGIN)
         taps = taps_ref[:, cols].astype(jnp.float32)
         band = jnp.zeros((2 * LANES, LANES), jnp.float32)
         for t in range(TAP_COUNT):
@@ -82,6 +82,81 @@
         return carry
 
     lax.fori_loop(0, bands.shape[0], step, 0)
+
+
+def plan_lines(src_ref, owner_ref, pair_cap, az, me, az_count, lines, recv_pick, tile_ref):
+    f32 = jnp.float32
+    count = src_ref.shape[1]
+    owned = tile_ref.shape[0]
+    owners = az_count * lax.axis_size("rg")
+    group_rows = 2 * pair_cap
+    groups = recv_pick.shape[0]
+    src = src_ref[...].astype(f32)
+    owner = owner_ref[...].astype(f32)
+    tile = jnp.zeros_like(src)
+    for a in range(1, az_count):
+        tile = tile + jnp.where(src >= a * lines, 1.0, 0.0)
+    az_f = az.astype(f32)
+    owner_is_me = owner == me.astype(f32)
+
+    def down(height, width):
+        return lax.broadcasted_iota(jnp.int32, (height, width), 0).astype(f32)
+
+    sent = jnp.where((down(owners, count) == owner) & (tile == az_f), 1.0, 0.0)
+    got = jnp.where((down(az_count, count) == tile) & owner_is_me, 1.0, 0.0)
+    own = jnp.broadcast_to(jnp.where(owner_is_me, 1.0, 0.0), (8, count))
+    hot = jnp.concatenate([sent, got, own], axis=0).astype(jnp.bfloat16)
+    ranks = []
+    for at in range(0, count, 2 * LANES):
+        before = lax.broadcasted_iota(jnp.int32, (count, 2 * LANES), 0)
+        after = lax.broadcasted_iota(jnp.int32, (count, 2 * LANES), 1) + at
+        earlier = jnp.where(before < after, 1.0, 0.0).astype(jnp.bfloat16)
+        ranks.append(dot(hot, earlier))
+    ranks = jnp.concatenate(ranks, axis=1)
+    sent_rank = jnp.sum(sent * ranks[:owners], axis=0, keepdims=True)
+    got_rank = jnp.sum(got * ranks[owners : owners + az_count], axis=0, keepdims=True)
+    own_rank = ranks[owners + az_count : owners + az_count + 1]
+
+    height = owners * (group_rows if group_rows == 8 else ROWS)
+    row = lax.broadcasted_iota(jnp.int32, (height, LANES), 0)
+    key = (row // (height // owners) * pair_cap + row % pair_cap).astype(f32)
+    slot = jnp.where(tile == az_f, owner * pair_cap + sent_rank, -1.0)
+    local = src - az_f * lines + 1.0
+    found = jnp.zeros((height, LANES), f32)
+    for at in range(0, count, LANES):
+        cols = slice(at, at + LANES)
+        found = found + jnp.where(slot[:, cols] == key, local[:, cols], 0.0)
+    found = jnp.sum(found, axis=1, keepdims=True)
+    row = lax.broadcasted_iota(jnp.int32, (height, 1), 0)
+    half = (row // pair_cap % 2).astype(f32)
+    target = jnp.where(found > 0.0, found - 1.0 + half * lines, -1.0)
+    across = lax.broadcasted_iota(jnp.int32, (height, 2 * lines), 1).astype(f32)
+    hit = jnp.where(across == target, 1.0, 0.0)
+    if group_rows == 8:
+        picks = [hit.astype(jnp.bfloat16)]
+    else:
+        group = row % ROWS // group_rows
+        picks = [jnp.where(group == g, hit, 0.0).astype(jnp.bfloat16) for g in range(groups)]
+
+    place = down(owned, LANES)
+    code = jnp.where(owner_is_me, tile * ROWS + got_rank + 1.0, 0.0)
+    found = jnp.zeros((owned, LANES), f32)
+    for at in range(0, count, LANES):
+        cols = slice(at, at + LANES)
+        found = found + jnp.where(own_rank[:, cols] == place, code[:, cols], 0.0)
+    found = jnp.sum(found, axis=1, keepdims=True)
+    from_tile = jnp.where(found > 0.0, 0.0, -1.0)
+    for a in range(1, az_count):
+        from_tile = from_tile + jnp.where(found > a * ROWS, 1.0, 0.0)
+    tile_ref[...] = jnp.broadcast_to(from_tile, tile_ref.shape)
+    across = lax.broadcasted_iota(jnp.int32, (owned, az_count * ROWS), 1).astype(f32)
+    for g in range(groups):
+        for p in range(2):
+            source = found - 1.0 + (g * group_rows + p * pair_cap)
+            source = jnp.where(found > 0.0, source, -1.0)
+            chosen = jnp.where(across == source, 1.0, 0.0).astype(jnp.bfloat16)
+            recv_pick[g, p * owned : (p + 1) * owned, :] = chosen
+    return picks
 
 
 def fill_windows(ref_ref, sec_ref, halos, ref_win, sec_win):
@@ -109,9 +184,9 @@
             sec_win[c, b, high:] = below[c].astype(f32)
 
 
-def estimate(off_ref, tables, base_ref, ref_win, sec_win, plain_ref, lagged_ref, est_ref):
+def estimate(off_ref, tables, base_ref, ref_win, sec_win, plain_ref, lagged_ref, est_ref, mine):
     four_ref, spec_ref, lift_ref, corr_ref, lag_ref, wide_ref = tables
-    chips = off_ref.shape[1]
+    chips = off_ref.shape[2]
     lines = sec_win.shape[2] - 2 * MARGIN
     rim = (CHIP_LEN - SPACING) // 2
     first = lines // 2 - CHIP_LEN // 2
@@ -141,8 +216,8 @@
             g = (i * GROUP + j) * 2
             at = [LANES + SPACING * (g + h) - rim for h in range(2)]
             ref_chips.append(pair(ref_win, (0, 0), at))
-            rows = [MARGIN + first + off_ref[0, g + h] for h in range(2)]
-            sec_chips.append(pair(sec_win, rows, [at[h] + off_ref[1, g + h] for h in range(2)]))
+            rows = [MARGIN + first + off_ref[0, 0, g + h] for h in range(2)]
+            sec_chips.append(pair(sec_win, rows, [at[h] + off_ref[1, 0, g + h] for h in range(2)]))
         both = jnp.concatenate(ref_chips + sec_chips, axis=1)
         half = dot(four_ref[...], both).astype(jnp.bfloat16)
         lhs = jnp.concatenate(
@@ -202,17 +277,21 @@
         for c, moment in enumerate((lagged, across)):
             centre = jnp.sum(jnp.where(inside, moment, 0.0), axis=1, keepdims=True) / total
             rows[c] = jnp.where(lane == place + h, centre, rows[c])
+    mine[...] = jnp.zeros_like(mine)
     for c in range(2):
-        est_ref[c : c + 1, :] = jnp.sum(rows[c], axis=0, keepdims=True) + base_ref[c : c + 1, :]
+        found = jnp.sum(rows[c], axis=0, keepdims=True)[:, :chips]
+        est_ref[c] = found + base_ref[c].astype(jnp.float32)
+    mine[:, :chips] = est_ref[0]
 
 
 def fused_kernel(
-    group_rows, far_first, off_ref, ref_ref, sec_ref, send_pick, recv_pick, rel_ref, taps_ref,
-    tile_ref, four_ref, spec_ref, lift_ref, corr_ref, lag_ref, wide_ref, base_ref, est_ref,
-    out_ref, outgoing, arrived, top, low, left, right, ref_left, ref_right, top_left, top_right,
-    low_left, low_right, ref_win, sec_win, plain_ref, lagged_ref, bands, wide, mine, everyone,
-    halo_send, halo_recv, bulk_send, bulk_recv, est_send, est_recv,
+    pair_cap, far_first, off_ref, base_ref, ref_ref, sec_ref, src_ref, owner_ref, start_ref,
+    taps_ref, four_ref, spec_ref, lift_ref, corr_ref, lag_ref, wide_ref, est_ref, out_ref,
+    recv_pick, tile_ref, outgoing, arrived, top, low, left, right, ref_left, ref_right, top_left,
+    top_right, low_left, low_right, ref_win, sec_win, plain_ref, lagged_ref, bands, wide, mine,
+    everyone, halo_send, halo_recv, bulk_send, bulk_recv, est_send, est_recv,
 ):
+    group_rows = 2 * pair_cap
     az_count = lax.axis_size("az")
     rg_count = lax.axis_size("rg")
     az = lax.axis_index("az")
@@ -243,20 +322,18 @@
 
     for_others(greet)
 
+    send_pick = plan_lines(
+        src_ref, owner_ref, pair_cap, az, me, az_count, lines, recv_pick, tile_ref
+    )
     rows = jnp.concatenate([sec_ref[0], sec_ref[1]], axis=0)
     for at in range(0, part, CHUNK):
         width = min(CHUNK, part - at)
         picked = [
-            dot(send_pick[g], rows[:, g * part + at : g * part + at + width])
-            for g in range(send_pick.shape[0])
+            dot(send_pick[g % len(send_pick)], rows[:, g * part + at : g * part + at + width])
+            for g in range(groups)
         ]
         if group_rows == 8:
-            picked = [
-                dot(send_pick[0], rows[:, g * part + at : g * part + at + width]).reshape(
-                    owners, group_rows, width
-                )
-                for g in range(groups)
-            ]
+            picked = [lines_g.reshape(owners, group_rows, width) for lines_g in picked]
             tall = jnp.concatenate(picked, axis=1)
         else:
             tall = sum(picked).reshape(owners, ROWS, width)
@@ -306,11 +383,17 @@
         def _():
             target[...] = jnp.zeros_like(target)
 
-    def bulk(d):
+    def partner(k):
+        quads = az_count // 4
+        turn_y = (az // 4 + k // 2) % quads
+        turn_x = (az // 2 + k // (2 * quads)) % 2
+        return (turn_y * 2 + turn_x) * 2 + (az + k) % 2
+
+    def bulk(d, low_k, high_k):
         to = (rg + d) % rg_count
 
         def one(k, carry):
-            a = (az + k) % az_count
+            a = partner(k)
             pltpu.make_async_remote_copy(
                 src_ref=outgoing.at[a * rg_count + to],
                 dst_ref=arrived.at[rg, az],
@@ -321,13 +404,14 @@
             ).start()
             return carry
 
-        lax.fori_loop(1 if d == 0 else 0, az_count, one, 0)
-
-    for d in far_first:
-        bulk(d)
+        lax.fori_loop(low_k, high_k, one, 0)
+
+    for low_k, high_k in ((0, az_count // 2), (az_count // 2, az_count)):
+        for d in far_first:
+            bulk(d, 1 if d == 0 and low_k == 0 else low_k, high_k)
     arrived[rg, az] = outgoing[az * rg_count + rg]
 
-    place_bands(rel_ref, taps_ref, bands)
+    place_bands(start_ref, taps_ref, bands)
 
     for which, (step_a, step_r, _, _) in enumerate(moves):
         @pl.when(inside(az - step_a, rg - step_r))
@@ -339,9 +423,10 @@
     )
     fill_windows(ref_ref, sec_ref, halos, ref_win, sec_win)
     tables = (four_ref, spec_ref, lift_ref, corr_ref, lag_ref, wide_ref)
-    estimate(off_ref, tables, base_ref, ref_win, sec_win, plain_ref, lagged_ref, est_ref)
-    mine[...] = est_ref[0:1, :]
-    everyone[me] = est_ref[0:1, :]
+    estimate(
+        off_ref, tables, base_ref, ref_win, sec_win, plain_ref, lagged_ref, est_ref, mine
+    )
+    everyone[me] = mine[...]
 
     def tell(a, r):
         pltpu.make_async_remote_copy(
@@ -433,34 +518,37 @@
     pltpu.make_async_copy(told, told, est_send).wait()
 
 
-def fused(offsets, ref, sec, send_pick, recv_pick, rel, taps, tile, tables, az_count, rg_count,
-          owner_cap, group_rows):
+def fused(offsets, ref, sec, src_row, line_owner, band_start, taps, tables, az_count, rg_count):
     four, spec, lift, corr, lags = tables
     lines = sec.shape[1]
     cols = sec.shape[2]
     chips = cols // SPACING
     blocks = cols // LANES
     owners = az_count * rg_count
-    part = cols * group_rows // ROWS
+    pair_cap = max(2, (lines + 2 * MAX_SHIFT + owners - 1) // owners)
+    owner_cap = pair_cap * az_count
+    groups = ROWS // (2 * pair_cap)
+    part = cols // groups
     far_first = sorted(range(1, rg_count), key=lambda d: abs(d - rg_count // 2)) + [0]
     vmem = pl.BlockSpec(memory_space=pltpu.VMEM)
     lag_wide = np.tile(np.pad(lags, (0, CHIP_LEN - LAG_COUNT)), 2)[None, :]
     bf16 = jnp.bfloat16
     f32 = jnp.float32
     args = (
-        offsets, ref, sec, send_pick, recv_pick, rel, taps, tile, four, spec, lift, corr,
-        jnp.asarray(lags)[:, None], jnp.asarray(lag_wide),
-        jnp.pad(offsets, ((0, 0), (0, LANES - chips))).astype(f32),
+        offsets, offsets, ref, sec, src_row[None], line_owner[None], band_start[None], taps,
+        four, spec, lift, corr, jnp.asarray(lags)[:, None], jnp.asarray(lag_wide),
     )
     return pl.pallas_call(
-        functools.partial(fused_kernel, group_rows, tuple(far_first)),
+        functools.partial(fused_kernel, pair_cap, tuple(far_first)),
         in_specs=[pl.BlockSpec(memory_space=pltpu.SMEM)] + [vmem] * (len(args) - 1),
         out_specs=(vmem, vmem),
         out_shape=(
-            jax.ShapeDtypeStruct((2, LANES), f32),
+            jax.ShapeDtypeStruct((2, 1, chips), f32),
             jax.ShapeDtypeStruct((2, owner_cap, cols * rg_count), bf16),
         ),
         scratch_shapes=[
+            pltpu.VMEM((groups, 2 * owner_cap, az_count * ROWS), bf16),
+            pltpu.VMEM((owner_cap, LANES), f32),
             pltpu.VMEM((owners, ROWS, part), bf16),
             pltpu.VMEM((rg_count, az_count, ROWS, part), bf16),
             pltpu.VMEM((2, MARGIN, cols), bf16),
@@ -498,73 +586,10 @@
 def per_device(
     reference_slc, secondary_slc, chip_offsets, src_row, line_owner, band_start, band_taps
 ):
-    tables = make_tables()
-    lines_dev = secondary_slc.shape[1]
-    cols_dev = secondary_slc.shape[2]
-    chip_count = cols_dev // SPACING
-    az_count = lax.axis_size("az")
-    rg_count = lax.axis_size("rg")
-    owners = az_count * rg_count
-    pair_cap = max(2, (lines_dev + 2 * MAX_SHIFT + owners - 1) // owners)
-    owner_cap = pair_cap * az_count
-    group_rows = 2 * pair_cap
-    groups = ROWS // group_rows
-    total_cols = cols_dev * rg_count
-    az_index = lax.axis_index("az")
-    rg_index = lax.axis_index("rg")
-    me_owner = az_index * rg_count + rg_index
-
-    count = src_row.shape[0]
-    ids = jnp.arange(count, dtype=jnp.int32)
-    src_tile = src_row // lines_dev
-    mine = (line_owner[:, None] == line_owner[None, :]) & (ids[:, None] < ids[None, :])
-    own_rank = jnp.sum(mine.astype(jnp.int32), axis=0)
-    near = mine & (src_tile[:, None] == src_tile[None, :])
-    pair_rank = jnp.sum(near.astype(jnp.int32), axis=0)
-
-    local_row = src_row - az_index * lines_dev
-    slot = jnp.where(src_tile == az_index, line_owner * pair_cap + pair_rank, -1)
-    slots = jnp.arange(owners * pair_cap, dtype=jnp.int32)
-    send_row = jnp.sum(
-        jnp.where(slots[:, None] == slot[None, :], local_row[None, :] + 1, 0), axis=1
-    ) - 1
-    send_row = send_row.reshape(owners, 1, pair_cap)
-    part = jnp.arange(2, dtype=jnp.int32)[None, :, None] * lines_dev
-    target = jnp.where(send_row >= 0, send_row + part, -1).reshape(owners, 1, group_rows)
-    if group_rows == 8:
-        target = target.reshape(1, owners * group_rows)
-    else:
-        group = jnp.arange(groups, dtype=jnp.int32)
-        at_group = group[:, None, None, None] == group[None, None, :, None]
-        target = jnp.where(at_group, target[None], -1).reshape(groups, owners * ROWS)
-    send_pick = (
-        target[:, :, None] == jnp.arange(2 * lines_dev, dtype=jnp.int32)[None, None, :]
-    ).astype(jnp.bfloat16)
-
-    all_cols = jnp.arange(total_cols, dtype=jnp.int32)
-    rel = (band_start - all_cols // LANES * LANES + MARGIN)[None, :]
-
-    outs = jnp.arange(owner_cap, dtype=jnp.int32)
-    placed = (own_rank[None, :] == outs[:, None]) & (line_owner == me_owner)[None, :]
-    which = jnp.sum(
-        jnp.where(placed, (src_tile * pair_cap + pair_rank + 1)[None, :], 0), axis=1
-    ) - 1
-    tile = which // pair_cap
-    from_rank = which % pair_cap
-    group = jnp.arange(groups, dtype=jnp.int32)[:, None, None]
-    parts = jnp.arange(2, dtype=jnp.int32)[None, :, None]
-    source = (tile * ROWS + from_rank)[None, None] + group * group_rows + parts * pair_cap
-    source = jnp.where(which[None, None] >= 0, source, -1).reshape(groups, 2 * owner_cap)
-    recv_pick = (
-        source[:, :, None] == jnp.arange(az_count * ROWS, dtype=jnp.int32)[None, None, :]
-    ).astype(jnp.bfloat16)
-    tile_wide = jnp.broadcast_to(tile[:, None], (owner_cap, LANES))
-
-    est, lines_out = fused(
-        chip_offsets[:, 0], reference_slc, secondary_slc, send_pick, recv_pick, rel, band_taps,
-        tile_wide, tables, az_count, rg_count, owner_cap, group_rows,
-    )
-    return (est[:, None, :chip_count], lines_out)
+    return fused(
+        chip_offsets, reference_slc, secondary_slc, src_row, line_owner, band_start, band_taps,
+        make_tables(), lax.axis_size("az"), lax.axis_size("rg"),
+    )
 
 
 def solution(mesh):

time: 71.9 us -> 62.5 us (0.87)
  other arithmetic: 7.91 us -> 0 us
  Pallas kernels: 57.8 us -> 55.2 us
  local copies, waits for them, and re-layouts: 5.09 us -> 6.4 us
    convert_element_type x3 -> x0, other arithmetic: 2.69 us -> none  [the longest x1 1.24 us: fused(): jnp.pad(offsets, ((0, 0), (0, LANES - chips))).astype(f32)]
    pallas_call x1, Pallas kernels: 57.8 us -> 55.2 us  [fused(): pl.pallas_call(functools.partial(fused_kernel, pair_cap, tuple(far_first)...]
    add x4 -> x0, other arithmetic: 2.24 us -> none  [the longest x1 1.43 us: per_device(): rel = (band_start - all_cols // LANES * LANES + MARGIN)[None, :]]
    broadcast_in_dim x3 -> x2, local copies, waits for them, and re-layouts: 0.76 us -> 2.54 us  [the longest x1 1.27 us: fused(): line_owner[None]]
    reduce_sum x3 -> x0, other arithmetic: 1.48 us -> none  [the longest x1 1.23 us: per_device(): own_rank = jnp.sum(mine.astype(jnp.int32), axis=0)]
    select_n x3 -> x0, other arithmetic: 0.79 us -> none  [the longest x1 0.7 us: per_device(): src_tile = src_row // lines_dev]
where the time goes in v1:
time: 62.5 us; the launch traced here: 62.3 us
  Pallas kernels  55.2 us (88%)
  local copies, waits for them, and re-layouts  6.4 us (10%)
  between operations  0.64 us (1%)
    pallas_call x1, Pallas kernels, fused(): pl.pallas_call(functools.partial(fused_kernel, pair_cap, tuple(far_first)...  55.2 us
    unnamed x2, local copies, waits for them, and re-layouts  3.87 us
    broadcast_in_dim x1, local copies, waits for them, and re-layouts, fused(): line_owner[None]  1.27 us
    broadcast_in_dim x1, local copies, waits for them, and re-layouts, fused(): src_row[None]  1.27 us

profile of v1, /device:TPU:0, one launch (start us, length us, event | category | flops | bytes accessed | tf_op | source)
XLA Modules:
  0.0 62.3 jit_solution(15657209697142368594)
XLA Ops:
  0.6 1.3 %broadcast_in_dim.12.src_ref = s32[1,768]{1,0:T(1,128)} reshape(s32[768]{0:T(1024)} %param.16) | data formatting | bytes 6144 | tf_op jit(solution)/shard_map/broadcast_in_dim | solution.py:538
  1.9 1.3 %broadcast_in_dim.13.owner_ref = s32[1,768]{1,0:T(1,128)} reshape(s32[768]{0:T(1024)} %param.17) | data formatting | bytes 6144 | tf_op jit(solution)/shard_map/broadcast_in_dim | solution.py:538
  3.2 55.2 %fused.1 = (f32[2,1,96]{2,1,0:T(1,128)}, bf16[2,32,12288]{2,1,0:T(8,128)(2,1)}) custom-call(s32[2,1,96]{2,1,0:T(1,128)} %base_ref.1, s32[2,1,96]{2,1,0:T(1,128)} %base_ref.1, bf16[2,96,3072]{2,1,0:T(8,128)(2,1)} %ref_ref.1, bf16[2,96,3072]{2,1,0:T(8,128)(2,1)} %sec_ref.1, s32[1,768]{1,0:T(1,128)} %broadcast_in_dim.12.src_ref, ...), custom_call_target="tpu_custom_call" | custom-call | tf_op jit(solution)/shard_map/fused/pallas_call | solution.py:541
  58.4 1.2 %copy.17 = f32[2,1,96]{2,1,0:T(1,128)} copy(f32[2,1,96]{2,1,0:T(1,128)} %get-tuple-element.4) | data formatting | bytes 1536
  59.6 2.7 %copy.18 = bf16[2,32,12288]{2,1,0:T(8,128)(2,1)} copy(bf16[2,32,12288]{2,1,0:T(8,128)(2,1)} %get-tuple-element.5) | data formatting | bytes 3145728

commit v2 on v1

--- a/solution.py
+++ b/solution.py
@@ -21,7 +21,7 @@
 
 PHASE_RATE = 2.0
 EPS = 1e-06
-VMEM_LIMIT = 56 * 1024 * 1024
+VMEM_LIMIT = 62 * 1024 * 1024
 
 
 def make_tables():
@@ -65,6 +65,7 @@
 
 
 ROWS = 16
+HOLD = 4
 CHUNK = 512
 
 
@@ -86,13 +87,13 @@
 
 def plan_lines(src_ref, owner_ref, pair_cap, az, me, az_count, lines, recv_pick, tile_ref):
     f32 = jnp.float32
-    count = src_ref.shape[1]
+    count = src_ref.shape[0]
     owned = tile_ref.shape[0]
     owners = az_count * lax.axis_size("rg")
     group_rows = 2 * pair_cap
     groups = recv_pick.shape[0]
-    src = src_ref[...].astype(f32)
-    owner = owner_ref[...].astype(f32)
+    src = src_ref[...].reshape(1, count).astype(f32)
+    owner = owner_ref[...].reshape(1, count).astype(f32)
     tile = jnp.zeros_like(src)
     for a in range(1, az_count):
         tile = tile + jnp.where(src >= a * lines, 1.0, 0.0)
@@ -279,18 +280,31 @@
             rows[c] = jnp.where(lane == place + h, centre, rows[c])
     mine[...] = jnp.zeros_like(mine)
     for c in range(2):
-        found = jnp.sum(rows[c], axis=0, keepdims=True)[:, :chips]
-        est_ref[c] = found + base_ref[c].astype(jnp.float32)
-    mine[:, :chips] = est_ref[0]
+        est_ref[c] = jnp.sum(rows[c], axis=0, keepdims=True)[:, :chips]
+    mine[:, :chips] = est_ref[0] + base_ref[0].astype(jnp.float32)
 
 
 def fused_kernel(
-    pair_cap, far_first, off_ref, base_ref, ref_ref, sec_ref, src_ref, owner_ref, start_ref,
-    taps_ref, four_ref, spec_ref, lift_ref, corr_ref, lag_ref, wide_ref, est_ref, out_ref,
-    recv_pick, tile_ref, outgoing, arrived, top, low, left, right, ref_left, ref_right, top_left,
-    top_right, low_left, low_right, ref_win, sec_win, plain_ref, lagged_ref, bands, wide, mine,
-    everyone, halo_send, halo_recv, bulk_send, bulk_recv, est_send, est_recv,
+    pair_cap, far_first, off_ref, src_hbm, owner_hbm, sec_hbm, ref_hbm, start_hbm, taps_hbm,
+    four_hbm, spec_hbm, lift_hbm, corr_hbm, lag_hbm, wide_hbm, base_hbm, est_ref, out_ref,
+    src_ref, owner_ref, sec_ref, ref_ref, start_ref, taps_ref, four_ref, spec_ref, lift_ref,
+    corr_ref, lag_ref, wide_ref, base_ref, recv_pick, tile_ref, outgoing, arrived, top, low, left,
+    right, ref_left, ref_right, top_left, top_right, low_left, low_right, ref_win, sec_win,
+    plain_ref, lagged_ref, bands, wide, mine, everyone, load_sem, halo_send, halo_recv, bulk_send,
+    bulk_recv, est_send, est_recv,
 ):
+    loads = [
+        pltpu.make_async_copy(source, target, load_sem.at[which])
+        for which, (source, target) in enumerate((
+            (src_hbm, src_ref), (owner_hbm, owner_ref), (sec_hbm, sec_ref), (ref_hbm, ref_ref),
+            (start_hbm, start_ref), (taps_hbm, taps_ref), (four_hbm, four_ref),
+            (spec_hbm, spec_ref), (lift_hbm, lift_ref), (corr_hbm, corr_ref),
+            (lag_hbm, lag_ref), (wide_hbm, wide_ref), (base_hbm, base_ref),
+        ))
+    ]
+    for load in loads:
+        load.start()
+
     group_rows = 2 * pair_cap
     az_count = lax.axis_size("az")
     rg_count = lax.axis_size("rg")
@@ -322,9 +336,12 @@
 
     for_others(greet)
 
+    loads[0].wait()
+    loads[1].wait()
     send_pick = plan_lines(
         src_ref, owner_ref, pair_cap, az, me, az_count, lines, recv_pick, tile_ref
     )
+    loads[2].wait()
     rows = jnp.concatenate([sec_ref[0], sec_ref[1]], axis=0)
     for at in range(0, part, CHUNK):
         width = min(CHUNK, part - at)
@@ -339,6 +356,7 @@
             tall = sum(picked).reshape(owners, ROWS, width)
         outgoing[:, :, at : at + width] = tall.astype(jnp.bfloat16)
 
+    loads[3].wait()
     pl.semaphore_wait(barrier, owners - 1)
 
     high = lines - MARGIN
@@ -406,11 +424,16 @@
 
         lax.fori_loop(low_k, high_k, one, 0)
 
-    for low_k, high_k in ((0, az_count // 2), (az_count // 2, az_count)):
-        for d in far_first:
-            bulk(d, 1 if d == 0 and low_k == 0 else low_k, high_k)
+    half = az_count // 2
+    groups_out = [(d, 1 if d == 0 else 0, half) for d in far_first]
+    groups_out += [(d, half, az_count) for d in far_first]
+    later = len(groups_out) - HOLD
+    for group in groups_out[:later]:
+        bulk(*group)
     arrived[rg, az] = outgoing[az * rg_count + rg]
 
+    for load in loads[4:]:
+        load.wait()
     place_bands(start_ref, taps_ref, bands)
 
     for which, (step_a, step_r, _, _) in enumerate(moves):
@@ -439,6 +462,8 @@
         ).start()
 
     for_others(tell)
+    for group in groups_out[later:]:
+        bulk(*group)
 
     owned = out_ref.shape[1]
     per_plane = cols // LANES
@@ -535,18 +560,19 @@
     bf16 = jnp.bfloat16
     f32 = jnp.float32
     args = (
-        offsets, offsets, ref, sec, src_row[None], line_owner[None], band_start[None], taps,
-        four, spec, lift, corr, jnp.asarray(lags)[:, None], jnp.asarray(lag_wide),
-    )
+        offsets, src_row, line_owner, sec, ref, band_start[None], taps, four, spec, lift, corr,
+        jnp.asarray(lags)[:, None], jnp.asarray(lag_wide), offsets,
+    )
+    hbm = pl.BlockSpec(memory_space=pltpu.HBM)
     return pl.pallas_call(
         functools.partial(fused_kernel, pair_cap, tuple(far_first)),
-        in_specs=[pl.BlockSpec(memory_space=pltpu.SMEM)] + [vmem] * (len(args) - 1),
+        in_specs=[pl.BlockSpec(memory_space=pltpu.SMEM)] + [hbm] * (len(args) - 1),
         out_specs=(vmem, vmem),
         out_shape=(
             jax.ShapeDtypeStruct((2, 1, chips), f32),
             jax.ShapeDtypeStruct((2, owner_cap, cols * rg_count), bf16),
         ),
-        scratch_shapes=[
+        scratch_shapes=[pltpu.VMEM(arg.shape, arg.dtype) for arg in args[1:]] + [
             pltpu.VMEM((groups, 2 * owner_cap, az_count * ROWS), bf16),
             pltpu.VMEM((owner_cap, LANES), f32),
             pltpu.VMEM((owners, ROWS, part), bf16),
@@ -569,6 +595,7 @@
             pltpu.VMEM((rg_count, 2 * owner_cap, cols + 2 * MARGIN), bf16),
             pltpu.VMEM((1, LANES), f32),
             pltpu.VMEM((owners, 1, LANES), f32),
+            pltpu.SemaphoreType.DMA((len(args) - 1,)),
             pltpu.SemaphoreType.DMA((10,)),
             pltpu.SemaphoreType.DMA((10,)),
             pltpu.SemaphoreType.DMA,
@@ -586,10 +613,11 @@
 def per_device(
     reference_slc, secondary_slc, chip_offsets, src_row, line_owner, band_start, band_taps
 ):
-    return fused(
+    shift, lines_out = fused(
         chip_offsets, reference_slc, secondary_slc, src_row, line_owner, band_start, band_taps,
         make_tables(), lax.axis_size("az"), lax.axis_size("rg"),
     )
+    return (chip_offsets.astype(jnp.float32) + shift, lines_out)
 
 
 def solution(mesh):

time: 62.5 us -> 55.1 us (0.88)
  Pallas kernels: 55.2 us -> 50.4 us
  local copies, waits for them, and re-layouts: 6.4 us -> 2.65 us
  other arithmetic: 0 us -> 1.22 us
    pallas_call x1, Pallas kernels: 55.2 us -> 50.4 us  [fused(): pl.pallas_call(functools.partial(fused_kernel, pair_cap, tuple(far_first)...]
    broadcast_in_dim x2 -> x0, local copies, waits for them, and re-layouts: 2.54 us -> none  [the longest x1 1.27 us: fused(): line_owner[None]]
    add x0 -> x1, other arithmetic: none -> 1.22 us  [per_device(): return (chip_offsets.astype(jnp.float32) + shift, lines_out)]
    unnamed x2 -> x3, local copies, waits for them, and re-layouts: 3.87 us -> 2.65 us
where the time goes in v2:
time: 55.1 us; the launch traced here: 54.9 us
  Pallas kernels  50.4 us (91%)
  local copies, waits for them, and re-layouts  2.65 us (5%)
  other arithmetic  1.22 us (2%)
  between operations  0.66 us (1%)
    pallas_call x1, Pallas kernels, fused(): pl.pallas_call(functools.partial(fused_kernel, pair_cap, tuple(far_first)...  50.4 us
    unnamed x3, local copies, waits for them, and re-layouts  2.65 us
    add x1, other arithmetic, per_device(): return (chip_offsets.astype(jnp.float32) + shift, lines_out)  1.22 us

profile of v2, /device:TPU:0, one launch (start us, length us, event | category | flops | bytes accessed | tf_op | source)
XLA Modules:
  0.0 54.9 jit_solution(14816988492715599775)
XLA Ops:
  0.6 0.0 copy-start
  0.6 50.4 %fused.1 = (f32[2,1,96]{2,1,0:T(1,128)}, bf16[2,32,12288]{2,1,0:T(8,128)(2,1)}) custom-call(s32[2,1,96]{2,1,0:T(1,128)} %base_hbm.1, s32[768]{0:T(1024)} %src_hbm.1, s32[768]{0:T(1024)} %owner_hbm.1, bf16[2,96,3072]{2,1,0:T(8,128)(2,1)} %sec_hbm.1, bf16[2,96,3072]{2,1,0:T(8,128)(2,1)} %ref_hbm.1, s32[1,12288]{1,0:T(1,128)} %bitcast.1, ...), custom_call_target="tpu_custom_call" | custom-call | tf_op jit(solution)/shard_map/fused/pallas_call | solution.py:567
  51.1 0.0 copy-done
  51.1 1.2 %convert_add_fusion = f32[2,1,96]{2,1,0:T(1,128)} fusion(f32[2,1,96]{2,1,0:T(1,128)} %get-tuple-element.4, s32[2,1,96]{2,1,0:T(1,128)S(1)} %copy-done), kind=kLoop, calls=%fused_computation | loop fusion | flops 384 | bytes 2304 | tf_op jit(solution)/shard_map/add | solution.py:620
  52.3 2.7 %copy.16 = bf16[2,32,12288]{2,1,0:T(8,128)(2,1)} copy(bf16[2,32,12288]{2,1,0:T(8,128)(2,1)} %get-tuple-element.9) | data formatting | bytes 3145728
Async XLA Ops:
  0.6 50.4 %copy-start = (s32[2,1,96]{2,1,0:T(1,128)S(1)}, s32[2,1,96]{2,1,0:T(1,128)}, u32[]{:S(2)}) copy-start(s32[2,1,96]{2,1,0:T(1,128)} %base_hbm.1) | copy-start | bytes 2308
